TPU v7x, 512 devices: a whole 4x8x8 slice. The times are simulated.
512 devices in a mesh: chan: 64 (over z, y_lo, x), facet: 8 (over y_hi, core).
Axes of the slice: x: 4, y: 8 (y_hi: 4, y_lo: 2; y = y_hi * 2 + y_lo), z: 8, core: 2. Of those that a mesh axis runs over, the one named last changes fastest.
Arguments:
- estimate: float32 [256, 128, 1024], P('chan', None, 'facet'), may hold values from -16 to 16
- dirty: float32 [256, 128, 1024], P('chan', None, 'facet'), may hold values from -16 to 16
- weights: float32 [256, 128, 1024], P('chan', None, 'facet'), may hold values from 0.2 to 1
- margin: int32 [8], replicated, may hold values from 1 to 16, as said below
- blend_table: int32 [8, 160], replicated, may hold values from 1 to 8
- tau_steps: int32 [2], replicated, may hold values from 1 to 4
Outputs:
- updated: float32 [256, 128, 1024], P('chan', None, 'facet')
Inputs may be any that keep to these rules, and one draw needn't show every extreme that they name: Some facet has margin exactly 16.
All inputs are finite; a program needn't handle non-finite values.
Results may differ from a plain program's by a relative error of at most 0.00012.
Values sent between devices are 32-bit elements; how exact they have to be, the bound alone decides.
No kernel may reach another device: no remote copies, remote signals or barrier semaphores. Data moves between devices by JAX's collectives and lax.ppermute only.
A program may use at most 64 MiB of HBM per device.

v0:
```python
import math
import jax
import jax.numpy as jnp
from jax import lax
from jax.sharding import PartitionSpec as P

OV = 16
NS_STEPS = 2
ITERS = 2


def padded(shard, sides, width):
    for axis, dim in sides:
        size, length = (lax.axis_size(axis), shard.shape[dim])
        up = [(i, (i + 1) % size) for i in range(size - 1)]
        down = [(j, i) for i, j in up]
        last = lax.slice_in_dim(shard, length - width, length, axis=dim)
        initial = lax.slice_in_dim(shard, 0, width, axis=dim)
        before = lax.ppermute(last, axis, up)
        after = lax.ppermute(initial, axis, down)
        shard = jnp.concatenate([before, shard, after], axis=dim)
    return shard


def apply_shrink(gram, columns, tau_value):
    channel_count = gram.shape[0]
    identity = jnp.eye(channel_count, dtype=jnp.float32)
    mean_eigen = jnp.trace(gram) / channel_count + 1e-06
    target = (gram + 0.01 * mean_eigen * identity) / (16.16 * mean_eigen)
    inverse_root = identity
    for newton_step in range(NS_STEPS):
        middle = 1.5 * identity - 0.5 * jnp.dot(
            inverse_root, target, precision=lax.Precision.HIGHEST
        )
        target = jnp.dot(target, middle, precision=lax.Precision.HIGHEST)
        inverse_root = jnp.dot(middle, inverse_root, precision=lax.Precision.HIGHEST)
    factor = 0.1 * tau_value / math.sqrt(1.01)
    kernel = identity - factor * inverse_root
    return jnp.dot(kernel, columns, precision=lax.Precision.HIGHEST)


def shrink_block(block, tau_value):
    columns = block.reshape(block.shape[0], -1)
    partial_value = jnp.dot(columns, columns.T, precision=lax.Precision.HIGHEST)
    gram = lax.psum(partial_value, "chan")
    return apply_shrink(gram, columns, tau_value).reshape(block.shape)


def extend(moved_cube):
    return padded(moved_cube, (("facet", 2),), OV)


def blend_sums(margin, blend_table, facet_id, facet_total, center):
    center_index = jnp.arange(center, dtype=jnp.int32)
    table_float = blend_table.astype(jnp.float32)
    own_part = table_float[facet_id][OV : OV + center]
    before_id = jnp.maximum(facet_id - 1, 0)
    after_id = jnp.minimum(facet_id + 1, facet_total - 1)
    before_slice = jnp.pad(table_float[before_id][center + OV :], (0, center - OV))
    after_slice = jnp.pad(table_float[after_id][:OV], (center - OV, 0))
    before_ok = (facet_id > 0) & (center_index < margin[before_id])
    after_ok = (facet_id < facet_total - 1) & (center_index >= center - margin[after_id])
    return (
        own_part + jnp.where(before_ok, before_slice, 0.0) + jnp.where(after_ok, after_slice, 0.0)
    )


def blend(result, row_weight, denominator, center):
    weighted = result * row_weight
    rims = jnp.concatenate([weighted[:, :, :OV], weighted[:, :, center + OV :]], axis=2)
    received = padded(rims, (("facet", 2),), OV)
    from_before = jnp.pad(received[:, :, :OV], ((0, 0), (0, 0), (0, center - OV)))
    from_after = jnp.pad(
        received[:, :, received.shape[2] - OV :], ((0, 0), (0, 0), (center - OV, 0))
    )
    core_rows = weighted[:, :, OV : OV + center] + from_before + from_after
    return core_rows / denominator


def per_device(estimate, dirty, weights, margin, blend_table, tau_steps):
    facet_id = lax.axis_index("facet")
    facet_total = lax.axis_size("facet")
    center = estimate.shape[2]
    ext_len = center + 2 * OV
    row_index = jnp.arange(ext_len, dtype=jnp.int32)
    own_width = margin[facet_id]
    keep_rows = ((row_index >= OV - own_width) & (row_index < center + OV + own_width)).astype(
        jnp.float32
    )
    row_weight = blend_table[facet_id].astype(jnp.float32) * keep_rows
    denominator = blend_sums(margin, blend_table, facet_id, facet_total, center)
    current = estimate
    for iteration in range(ITERS):
        tau_value = tau_steps[iteration].astype(jnp.float32)
        moved_cube = current - weights * (current - dirty)
        extended = extend(moved_cube) * keep_rows
        pixel_view = lax.all_to_all(extended, "chan", split_axis=1, concat_axis=0, tiled=True)
        result = shrink_block(pixel_view, tau_value)
        back_view = lax.all_to_all(result, "chan", split_axis=0, concat_axis=1, tiled=True)
        current = blend(back_view, row_weight, denominator, center)
    return current


def solution(mesh):
    placed = (
        P("chan", None, "facet"),
        P("chan", None, "facet"),
        P("chan", None, "facet"),
        P(),
        P(),
        P(),
    )
    return jax.shard_map(
        per_device, mesh=mesh, in_specs=placed, out_specs=P("chan", None, "facet"), check_vma=False
    )
```

profile of v0, /device:TPU:1, one launch (start us, length us, event | category | flops | bytes accessed | tf_op | source)
XLA Modules:
  0.0 1311.3 jit_solution(14268849020404267029)
XLA Ops:
  6.5 1.1 multiply_subtract_fusion.1
  7.8 5.6 collective-permute-start
  13.4 4.5 collective-permute-start.1
  17.9 0.6 copy-done.5
  18.6 0.7 fusion.28
  20.5 4.3 collective-permute-done.1
  25.4 26.8 %all_to_all.66 = f32[4,128,160]{2,0,1:T(4,128)S(1)} all-to-all(f32[4,128,160]{2,0,1:T(4,128)S(1)} %copy.53), channel_id=1, replica_groups=mesh['chan'=64,'facet'=8] {'chan'}, dimensions={1} | all-to-all | bytes 655360 | tf_op jit(solution)/shard_map/all_to_all | solution.py:97
  53.0 1.3 fusion.29
  56.3 531.9 %all-reduce.9.cloned.1.call-done = f32[256,256]{1,0:T(8,128)} async-done(((f32[256,256]{1,0:T(8,128)}), f32[256,256]{1,0:T(8,128)}) %all-reduce.9.cloned.1.call-update) | async-done | bytes 262160 | tf_op jit(solution)/shard_map/psum | solution.py:45
  588.3 1.7 select_reduce_fusion.1
  592.9 1.0 copy.56
  593.9 9.1 all-to-all-start.1
  604.5 11.8 all-to-all-done.1
  616.7 35.2 %collective-permute-start.2 = (f32[4,128,16]{2,1,0:T(8,128)S(1)}, f32[4,128,16]{2,1,0:T(8,128)S(1)}, u32[]{:S(2)}, u32[]{:S(2)}) collective-permute-start(f32[4,128,16]{2,1,0:T(8,128)S(1)} %get-tuple-element.7), channel_id=1, source_target_pairs={{0,1},{1,2},{2,3},{3,4},{4,5},{5,6},{6,7},{8,9},{9,10},{10,11},{11... | collective-permute-start | bytes 98312 | tf_op jit(solution)/shard_map/ppermute | solution.py:19
  651.9 1.9 collective-permute-start.3
  653.8 0.7 fusion.17
  654.5 0.7 collective-permute-done.2
  655.2 8.1 collective-permute-done.3
  663.6 1.9 collective-permute-start.4
  665.6 2.4 collective-permute-start.5
  668.0 0.9 collective-permute-done.4
  668.9 7.9 collective-permute-done.5
  677.5 18.4 %all_to_all.67 = f32[4,128,160]{2,0,1:T(4,128)S(1)} all-to-all(f32[4,128,160]{2,0,1:T(4,128)S(1)} %copy.59), channel_id=1, replica_groups=mesh['chan'=64,'facet'=8] {'chan'}, dimensions={1} | all-to-all | bytes 655360 | tf_op jit(solution)/shard_map/all_to_all | solution.py:97
  696.6 1.3 fusion.31
  698.7 530.9 %all-reduce.11.cloned.1.call-done = f32[256,256]{1,0:T(8,128)} async-done(((f32[256,256]{1,0:T(8,128)}), f32[256,256]{1,0:T(8,128)}) %all-reduce.11.cloned.1.call-update) | async-done | bytes 262160 | tf_op jit(solution)/shard_map/psum | solution.py:45
  1229.6 1.7 select_reduce_fusion
  1234.4 22.2 %all_to_all.68 = f32[256,2,160]{2,1,0:T(2,128)S(1)} all-to-all(f32[256,2,160]{2,1,0:T(2,128)S(1)} %copy.62), channel_id=1, replica_groups=mesh['chan'=64,'facet'=8] {'chan'}, dimensions={0} | all-to-all | bytes 655360 | tf_op jit(solution)/shard_map/all_to_all | solution.py:99
  1257.0 35.2 %collective-permute-start.6 = (f32[4,128,16]{2,1,0:T(8,128)S(1)}, f32[4,128,16]{2,1,0:T(8,128)S(1)}, u32[]{:S(2)}, u32[]{:S(2)}) collective-permute-start(f32[4,128,16]{2,1,0:T(8,128)S(1)} %get-tuple-element.5), channel_id=1, source_target_pairs={{0,1},{1,2},{2,3},{3,4},{4,5},{5,6},{6,7},{8,9},{9,10},{10,11},{11... | collective-permute-start | bytes 98312 | tf_op jit(solution)/shard_map/ppermute | solution.py:19
  1292.2 1.9 collective-permute-start.7
  1294.1 1.4 collective-permute-done.6
  1295.5 8.1 collective-permute-done.7
  1303.6 0.9 fusion.9
  (56 shorter events, 10.9 us)
Async XLA Ops:
  6.5 581.7 %all-reduce.9.cloned.1.call-start = ((), (), s32[]{:S(2)}) async-start(), calls=%async_computation.4 | async-start | bytes 524288 | tf_op jit(solution)/shard_map/psum | solution.py:45
  7.8 12.7 collective-permute-start
  13.4 11.4 collective-permute-start.1
  17.9 0.7 copy-start.5
  54.3 0.7 copy-start.6
  588.3 2.3 copy-start.3
  593.9 22.4 %all-to-all-start.1 = ((f32[256,2,160]{2,1,0:T(2,128)}), f32[256,2,160]{2,1,0:T(2,128)S(1)}, u32[]{:S(2)}, u32[]{:S(2)}) async-start(f32[256,2,160]{2,1,0:T(2,128)} %copy.56), calls=%async_computation.1 | async-start | bytes 1048576 | tf_op jit(solution)/shard_map/all_to_all | solution.py:99
  603.1 0.7 copy-start.4
  603.1 626.5 %all-reduce.11.cloned.1.call-start = ((), (), s32[]{:S(2)}) async-start(), calls=%async_computation.5 | async-start | bytes 524288 | tf_op jit(solution)/shard_map/psum | solution.py:45
  616.6 46.7 %copy-start = (f32[4,128,128]{2,1,0:T(8,128)S(1)}, f32[4,128,128]{2,1,0:T(8,128)}, u32[]{:S(2)}) copy-start(f32[4,128,128]{2,1,0:T(8,128)} %param.8) | copy-start | bytes 786436
  616.6 46.7 %copy-start.1 = (f32[4,128,128]{2,1,0:T(8,128)S(1)}, f32[4,128,128]{2,1,0:T(8,128)}, u32[]{:S(2)}) copy-start(f32[4,128,128]{2,1,0:T(8,128)} %param.7) | copy-start | bytes 786436
  616.7 38.5 %collective-permute-start.2 = (f32[4,128,16]{2,1,0:T(8,128)S(1)}, f32[4,128,16]{2,1,0:T(8,128)S(1)}, u32[]{:S(2)}, u32[]{:S(2)}) collective-permute-start(f32[4,128,16]{2,1,0:T(8,128)S(1)} %get-tuple-element.7), channel_id=1, source_target_pairs={{0,1},{1,2},{2,3},{3,4},{4,5},{5,6},{6,7},{8,9},{9,10},{10,11},{11... | collective-permute-start | bytes 98312 | tf_op jit(solution)/shard_map/ppermute | solution.py:19
  651.9 11.4 collective-permute-start.3
  663.6 5.3 collective-permute-start.4
  665.6 11.3 collective-permute-start.5
  1229.6 2.3 copy-start.2
  1257.0 38.5 %collective-permute-start.6 = (f32[4,128,16]{2,1,0:T(8,128)S(1)}, f32[4,128,16]{2,1,0:T(8,128)S(1)}, u32[]{:S(2)}, u32[]{:S(2)}) collective-permute-start(f32[4,128,16]{2,1,0:T(8,128)S(1)} %get-tuple-element.5), channel_id=1, source_target_pairs={{0,1},{1,2},{2,3},{3,4},{4,5},{5,6},{6,7},{8,9},{9,10},{10,11},{11... | collective-permute-start | bytes 98312 | tf_op jit(solution)/shard_map/ppermute | solution.py:19
  1292.2 11.4 collective-permute-start.7
Sparse Core Ops, SparseCore 0:
  54.4 533.8 all-reduce.8
  698.1 531.4 all-reduce.10
where the time goes:
time: 1310 us
  waiting for transfers between devices  1110 us (85%)
  starting transfers between devices  97.7 us (7%)
  blocking collectives  67.4 us (5%)
  between operations  18.3 us (1%)
    psum x2, waiting for transfers between devices, shrink_block(): gram = lax.psum(partial_value, 'chan')  1060 us
    ppermute x4, starting transfers between devices, padded(): before = lax.ppermute(last, axis, up)  77.8 us
    all_to_all x2, blocking collectives, per_device(): lax.all_to_all(extended, 'chan', split_axis=1, concat_axis=0, tiled=True)  45.2 us
    ppermute x4, waiting for transfers between devices, padded(): after = lax.ppermute(initial, axis, down)  28.3 us
  transfers between devices with their start and end apart: 11, of which 10 were waited for; matrix products, arithmetic and copies ran while one was open for 0% of the time, Pallas kernels for 0%

commit v1 on v0

--- a/solution.py
+++ b/solution.py
@@ -42,7 +42,7 @@
 def shrink_block(block, tau_value):
     columns = block.reshape(block.shape[0], -1)
     partial_value = jnp.dot(columns, columns.T, precision=lax.Precision.HIGHEST)
-    gram = lax.psum(partial_value, "chan")
+    gram = jnp.sum(lax.all_gather(partial_value, "chan"), axis=0)
     return apply_shrink(gram, columns, tau_value).reshape(block.shape)
 
 

time: 1310 us -> 856 us (0.65)
  waiting for transfers between devices: 1110 us -> 616 us
  starting transfers between devices: 97.7 us -> 123 us
    psum x2 -> x0, waiting for transfers between devices: 1060 us -> none  [shrink_block(): gram = lax.psum(partial_value, 'chan')]
    all_gather x0 -> x2, waiting for transfers between devices: none -> 572 us  [shrink_block(): gram = jnp.sum(lax.all_gather(partial_value, 'chan'), axis=0)]
    ppermute x4, starting transfers between devices: 77.8 us -> 105 us  [padded(): before = lax.ppermute(last, axis, up)]
    reduce_sum x0 -> x2, other arithmetic: none -> 13.7 us  [shrink_block(): gram = jnp.sum(lax.all_gather(partial_value, 'chan'), axis=0)]
where the time goes in v1:
time: 856 us; the launch traced here: 855 us
  waiting for transfers between devices  616 us (72%)
  starting transfers between devices  123 us (14%)
  blocking collectives  65 us (8%)
  other arithmetic  18.6 us (2%)
  between operations  18.2 us (2%)
    all_gather x2, waiting for transfers between devices, shrink_block(): gram = jnp.sum(lax.all_gather(partial_value, 'chan'), axis=0)  572 us
    ppermute x4, starting transfers between devices, padded(): before = lax.ppermute(last, axis, up)  105 us
    all_to_all x2, blocking collectives, per_device(): lax.all_to_all(extended, 'chan', split_axis=1, concat_axis=0, tiled=True)  46.7 us
    ppermute x4, waiting for transfers between devices, padded(): after = lax.ppermute(initial, axis, down)  27.7 us
    all_to_all x1, blocking collectives, per_device(): lax.all_to_all(result, 'chan', split_axis=0, concat_axis=1, tiled=True)  18.3 us
  transfers between devices with their start and end apart: 11, of which 10 were waited for; matrix products, arithmetic and copies ran while one was open for 0% of the time, Pallas kernels for 0%

profile of v1, /device:TPU:1, one launch (start us, length us, event | category | flops | bytes accessed | tf_op | source)
XLA Modules:
  0.0 854.9 jit_solution(7561027718314809898)
XLA Ops:
  6.5 1.1 multiply_subtract_fusion.1
  7.8 5.6 collective-permute-start
  13.4 4.5 collective-permute-start.1
  17.9 1.4 fusion.28
  20.6 4.2 collective-permute-done.1
  25.5 26.9 %all_to_all.66 = f32[4,128,160]{2,0,1:T(4,128)S(1)} all-to-all(f32[4,128,160]{2,0,1:T(4,128)S(1)} %copy.53), channel_id=1, replica_groups=mesh['chan'=64,'facet'=8] {'chan'}, dimensions={1} | all-to-all | bytes 655360 | tf_op jit(solution)/shard_map/all_to_all | solution.py:97
  53.1 1.3 fusion.29
  54.5 1.4 fusion.27
  56.6 285.9 %all-gather.5.cloned.1.call-done = f32[16384,256]{1,0:T(8,128)} async-done(((f32[256,256]{1,0:T(8,128)}), f32[16384,256]{1,0:T(8,128)}) %all-gather.5.cloned.1.call-update) | async-done | bytes 16777232 | tf_op jit(solution)/shard_map/all_gather | solution.py:45
  342.5 6.8 reduce_sum.34
  352.9 1.0 copy.56
  353.9 7.0 all-to-all-start.1
  361.7 12.8 %all-to-all-done.1 = f32[256,2,160]{2,1,0:T(2,128)S(1)} async-done(((f32[256,2,160]{2,1,0:T(2,128)}), f32[256,2,160]{2,1,0:T(2,128)S(1)}, u32[]{:S(2)}, u32[]{:S(2)}) %all-to-all-start.1) | async-done | bytes 327712 | tf_op jit(solution)/shard_map/all_to_all | solution.py:99
  374.9 48.4 %collective-permute-start.2 = (f32[4,128,16]{2,1,0:T(8,128)S(1)}, f32[4,128,16]{2,1,0:T(8,128)S(1)}, u32[]{:S(2)}, u32[]{:S(2)}) collective-permute-start(f32[4,128,16]{2,1,0:T(8,128)S(1)} %get-tuple-element.7), channel_id=1, source_target_pairs={{0,1},{1,2},{2,3},{3,4},{4,5},{5,6},{6,7},{8,9},{9,10},{10,11},{11... | collective-permute-start | bytes 98312 | tf_op jit(solution)/shard_map/ppermute | solution.py:19
  423.3 1.9 collective-permute-start.3
  425.2 0.6 fusion.17
  425.9 0.8 collective-permute-done.2
  426.7 8.1 collective-permute-done.3
  435.1 1.9 collective-permute-start.4
  437.0 2.4 collective-permute-start.5
  439.4 0.9 collective-permute-done.4
  440.3 7.4 collective-permute-done.5
  448.3 19.7 %all_to_all.67 = f32[4,128,160]{2,0,1:T(4,128)S(1)} all-to-all(f32[4,128,160]{2,0,1:T(4,128)S(1)} %copy.59), channel_id=1, replica_groups=mesh['chan'=64,'facet'=8] {'chan'}, dimensions={1} | all-to-all | bytes 655360 | tf_op jit(solution)/shard_map/all_to_all | solution.py:97
  468.8 1.3 fusion.31
  470.9 286.1 %all-gather.7.cloned.1.call-done = f32[16384,256]{1,0:T(8,128)} async-done(((f32[256,256]{1,0:T(8,128)}), f32[16384,256]{1,0:T(8,128)}) %all-gather.7.cloned.1.call-update) | async-done | bytes 16777232 | tf_op jit(solution)/shard_map/all_gather | solution.py:45
  757.0 6.8 reduce_sum.36
  767.6 18.3 %all_to_all.68 = f32[256,2,160]{2,1,0:T(2,128)S(1)} all-to-all(f32[256,2,160]{2,1,0:T(2,128)S(1)} %copy.62), channel_id=1, replica_groups=mesh['chan'=64,'facet'=8] {'chan'}, dimensions={0} | all-to-all | bytes 655360 | tf_op jit(solution)/shard_map/all_to_all | solution.py:99
  786.3 49.4 %collective-permute-start.6 = (f32[4,128,16]{2,1,0:T(8,128)S(1)}, f32[4,128,16]{2,1,0:T(8,128)S(1)}, u32[]{:S(2)}, u32[]{:S(2)}) collective-permute-start(f32[4,128,16]{2,1,0:T(8,128)S(1)} %get-tuple-element.5), channel_id=1, source_target_pairs={{0,1},{1,2},{2,3},{3,4},{4,5},{5,6},{6,7},{8,9},{9,10},{10,11},{11... | collective-permute-start | bytes 98312 | tf_op jit(solution)/shard_map/ppermute | solution.py:19
  835.7 1.9 collective-permute-start.7
  837.6 1.4 collective-permute-done.6
  839.1 8.1 collective-permute-done.7
  847.1 0.9 fusion.9
  (50 shorter events, 10.3 us)
Async XLA Ops:
  6.5 335.9 %all-gather.5.cloned.1.call-start = ((), (), s32[]{:S(2)}) async-start(), calls=%async_computation.4 | async-start | bytes 17039360 | tf_op jit(solution)/shard_map/all_gather | solution.py:45
  7.7 353.2 %copy-start.2 = (s32[8,160]{1,0:T(8,128)S(1)}, s32[8,160]{1,0:T(8,128)}, u32[]{:S(2)}) copy-start(s32[8,160]{1,0:T(8,128)} %param.10) | copy-start | bytes 15364
  7.8 12.8 %collective-permute-start = (f32[4,128,16]{2,1,0:T(8,128)S(1)}, f32[4,128,16]{2,1,0:T(8,128)S(1)}, u32[]{:S(2)}, u32[]{:S(2)}) collective-permute-start(f32[4,128,16]{2,1,0:T(8,128)S(1)} %get-tuple-element.11), channel_id=1, source_target_pairs={{0,1},{1,2},{2,3},{3,4},{4,5},{5,6},{6,7},{8,9},{9,10},{10,11},{11... | collective-permute-start | bytes 98312 | tf_op jit(solution)/shard_map/ppermute | solution.py:19
  13.4 11.4 %collective-permute-start.1 = (f32[4,128,16]{2,1,0:T(8,128)S(1)}, f32[4,128,16]{2,1,0:T(8,128)S(1)}, u32[]{:S(2)}, u32[]{:S(2)}) collective-permute-start(f32[4,128,16]{2,1,0:T(8,128)S(1)} %get-tuple-element.12), channel_id=1, source_target_pairs={{1,0},{2,1},{3,2},{4,3},{5,4},{6,5},{7,6},{9,8},{10,9},{11,10},{12... | collective-permute-start | bytes 98312 | tf_op jit(solution)/shard_map/ppermute | solution.py:20
  25.5 409.2 %copy-start = (f32[4,128,128]{2,1,0:T(8,128)S(1)}, f32[4,128,128]{2,1,0:T(8,128)}, u32[]{:S(2)}) copy-start(f32[4,128,128]{2,1,0:T(8,128)} %param.8) | copy-start | bytes 786436
  25.5 409.2 %copy-start.1 = (f32[4,128,128]{2,1,0:T(8,128)S(1)}, f32[4,128,128]{2,1,0:T(8,128)}, u32[]{:S(2)}) copy-start(f32[4,128,128]{2,1,0:T(8,128)} %param.7) | copy-start | bytes 786436
  353.9 20.6 %all-to-all-start.1 = ((f32[256,2,160]{2,1,0:T(2,128)}), f32[256,2,160]{2,1,0:T(2,128)S(1)}, u32[]{:S(2)}, u32[]{:S(2)}) async-start(f32[256,2,160]{2,1,0:T(2,128)} %copy.56), calls=%async_computation.1 | async-start | bytes 1048576 | tf_op jit(solution)/shard_map/all_to_all | solution.py:99
  360.9 396.1 %all-gather.7.cloned.1.call-start = ((), (), s32[]{:S(2)}) async-start(), calls=%async_computation.5 | async-start | bytes 17039360 | tf_op jit(solution)/shard_map/all_gather | solution.py:45
  374.9 51.8 %collective-permute-start.2 = (f32[4,128,16]{2,1,0:T(8,128)S(1)}, f32[4,128,16]{2,1,0:T(8,128)S(1)}, u32[]{:S(2)}, u32[]{:S(2)}) collective-permute-start(f32[4,128,16]{2,1,0:T(8,128)S(1)} %get-tuple-element.7), channel_id=1, source_target_pairs={{0,1},{1,2},{2,3},{3,4},{4,5},{5,6},{6,7},{8,9},{9,10},{10,11},{11... | collective-permute-start | bytes 98312 | tf_op jit(solution)/shard_map/ppermute | solution.py:19
  423.3 11.4 %collective-permute-start.3 = (f32[4,128,16]{2,1,0:T(8,128)S(1)}, f32[4,128,16]{2,1,0:T(8,128)S(1)}, u32[]{:S(2)}, u32[]{:S(2)}) collective-permute-start(f32[4,128,16]{2,1,0:T(8,128)S(1)} %get-tuple-element.8), channel_id=1, source_target_pairs={{1,0},{2,1},{3,2},{4,3},{5,4},{6,5},{7,6},{9,8},{10,9},{11,10},{12... | collective-permute-start | bytes 98312 | tf_op jit(solution)/shard_map/ppermute | solution.py:20
  435.1 5.3 collective-permute-start.4
  437.0 10.7 %collective-permute-start.5 = (f32[4,128,16]{2,1,0:T(8,128)S(1)}, f32[4,128,16]{2,1,0:T(8,128)S(1)}, u32[]{:S(2)}, u32[]{:S(2)}) collective-permute-start(f32[4,128,16]{2,1,0:T(8,128)S(1)} %get-tuple-element.10), channel_id=1, source_target_pairs={{1,0},{2,1},{3,2},{4,3},{5,4},{6,5},{7,6},{9,8},{10,9},{11,10},{12... | collective-permute-start | bytes 98312 | tf_op jit(solution)/shard_map/ppermute | solution.py:20
  786.3 52.8 %collective-permute-start.6 = (f32[4,128,16]{2,1,0:T(8,128)S(1)}, f32[4,128,16]{2,1,0:T(8,128)S(1)}, u32[]{:S(2)}, u32[]{:S(2)}) collective-permute-start(f32[4,128,16]{2,1,0:T(8,128)S(1)} %get-tuple-element.5), channel_id=1, source_target_pairs={{0,1},{1,2},{2,3},{3,4},{4,5},{5,6},{6,7},{8,9},{9,10},{10,11},{11... | collective-permute-start | bytes 98312 | tf_op jit(solution)/shard_map/ppermute | solution.py:19
  835.7 11.4 %collective-permute-start.7 = (f32[4,128,16]{2,1,0:T(8,128)S(1)}, f32[4,128,16]{2,1,0:T(8,128)S(1)}, u32[]{:S(2)}, u32[]{:S(2)}) collective-permute-start(f32[4,128,16]{2,1,0:T(8,128)S(1)} %get-tuple-element.6), channel_id=1, source_target_pairs={{1,0},{2,1},{3,2},{4,3},{5,4},{6,5},{7,6},{9,8},{10,9},{11,10},{12... | collective-permute-start | bytes 98312 | tf_op jit(solution)/shard_map/ppermute | solution.py:20
Sparse Core Ops, SparseCore 0:
  54.6 287.8 all-gather.4
  470.2 286.6 all-gather.6
